TPU v7x, 32 devices: a whole 2x2x4 slice. The times are simulated.
32 devices in a mesh: groups: 2 (over y), shard: 4 (over z), dp: 2 (over x), tok: 2 (over core).
Axes of the slice: x: 2, y: 2, z: 4, core: 2. Of those that a mesh axis runs over, the one named last changes fastest.
Arguments:
- tokens: bfloat16 [2048, 4096], P(('groups', 'dp', 'tok'), 'shard'), parts along dimension 0, may hold values from -6 to 6
- gate_blocks: bfloat16 [8, 16, 128, 128], P('shard'), may hold values from -0.125 to 0.125
- up_blocks: bfloat16 [8, 16, 128, 128], P('shard'), may hold values from -0.125 to 0.125
- down_blocks: bfloat16 [8, 16, 128, 128], P('shard'), may hold values from -0.25 to 0.25
- gate_rows: int32 [8, 16], P('shard'), may hold values from 0 to 31, as said below
- up_rows: int32 [8, 16], P('shard'), may hold values from 0 to 31, as said below
- down_rows: int32 [8, 16], replicated, may hold values from 0 to 31, as said below
- cotangent: bfloat16 [2048, 4096], P(('groups', 'dp', 'tok'), 'shard'), parts along dimension 0, may hold values from -6 to 6
Outputs:
- mixed: bfloat16 [2048, 4096], P(('groups', 'dp', 'tok'), 'shard'), parts along dimension 0
- tokens_grad: bfloat16 [2048, 4096], P(('groups', 'dp', 'tok'), 'shard'), parts along dimension 0
- gate_grad: bfloat16 [16, 16, 128, 128], P(('groups', 'shard'), ('dp', 'tok')), parts along dimension 0
- up_grad: bfloat16 [16, 16, 128, 128], P(('groups', 'shard'), ('dp', 'tok')), parts along dimension 0
- down_grad: bfloat16 [16, 16, 128, 128], P(('groups', 'shard'), ('dp', 'tok')), parts along dimension 0
There are 2 independent parts, one for each index of `groups`. A program takes and returns all parts, laid end to end along the dimension named above; an argument that names none is the same for every part. Nothing has to cross between parts.
Inputs may be any that keep to these rules, and one draw needn't show every extreme that they name: `gate_rows`: in every row c of the list and for every o, the entries o * 4 to (o + 1) * 4 - 1 are distinct blocks among o * 2 * 4 to (o + 1) * 2 * 4 - 1, in ascending order. `up_rows`: as for gate_rows, drawn independently. `down_rows`: as for gate_rows, drawn independently.
All inputs are finite; a program needn't handle non-finite values.
Results may differ from a plain program's by a relative error of at most 0.018.
Values may be sent and summed in bfloat16 or wider, within the bound.
No kernel may reach another device: no remote copies, remote signals or barrier semaphores. Data moves between devices by JAX's collectives and lax.ppermute only.
A program may use at most 64 MiB of HBM per device.

v0:
```python
import jax
import jax.numpy as jnp
from jax import lax
from jax.sharding import PartitionSpec as P


def body(tokens, gate_blocks, up_blocks, down_blocks, gate_rows, up_rows, down_rows, cotangent):
    shard_count = lax.axis_size("shard")
    owner_index = lax.axis_index("shard")
    token_count = tokens.shape[0]
    owned_width = tokens.shape[1]
    column_count = gate_blocks.shape[0]
    nonzero = gate_blocks.shape[1]
    block_size = gate_blocks.shape[2]
    owned_blocks = owned_width // block_size
    per_owner = nonzero // shard_count
    gathered = lax.all_gather(tokens, "shard", axis=1, tiled=True)
    row_blocks = gathered.shape[1] // block_size
    tokens3 = gathered.reshape(token_count, row_blocks, block_size)
    gate_in = jnp.take(tokens3, gate_rows, axis=1)
    up_in = jnp.take(tokens3, up_rows, axis=1)
    gate = jnp.einsum("nckb,ckbh->nch", gate_in, gate_blocks, preferred_element_type=jnp.float32)
    up = jnp.einsum("nckb,ckbh->nch", up_in, up_blocks, preferred_element_type=jnp.float32)
    hidden = (jax.nn.silu(gate) * up).astype(jnp.bfloat16)
    out_blocks = jnp.einsum(
        "nch,ckho->ncko", hidden, down_blocks, preferred_element_type=jnp.float32
    ).astype(jnp.bfloat16)
    sending = out_blocks.reshape(token_count, column_count, shard_count, per_owner * block_size)
    received = lax.all_to_all(sending, "shard", split_axis=2, concat_axis=2, tiled=True)
    received5 = received.reshape(token_count, column_count, shard_count, per_owner, block_size)
    owner_cols = lax.dynamic_slice_in_dim(down_rows, owner_index * per_owner, per_owner, 1)
    local_rows = (
        owner_cols.reshape(shard_count, column_count, per_owner) - owner_index * owned_blocks
    )
    one_hot = (
        local_rows[:, :, :, None] == jnp.arange(owned_blocks, dtype=jnp.int32)[None, None, None, :]
    ).astype(jnp.bfloat16)
    mixed_rows = jnp.einsum(
        "ncsjb,scjr->nrb", received5, one_hot, preferred_element_type=jnp.float32
    )
    mixed = mixed_rows.reshape(token_count, owned_width).astype(jnp.bfloat16)
    own_cot = cotangent.reshape(token_count, owned_blocks, block_size)
    picked = jnp.take(own_cot, local_rows.reshape(shard_count * column_count * per_owner), axis=1)
    outgoing = picked.reshape(token_count, shard_count, column_count * per_owner * block_size)
    incoming = lax.all_to_all(outgoing, "shard", split_axis=1, concat_axis=1, tiled=True)
    cot_five = incoming.reshape(token_count, shard_count, column_count, per_owner, block_size)
    cot_form = "nocjb"
    down_five = down_blocks.reshape(column_count, shard_count, per_owner, block_size, block_size)
    hidden_grad = jnp.einsum(
        cot_form + ",cojhb->nch", cot_five, down_five, preferred_element_type=jnp.float32
    )
    sigmoid_gate = jax.nn.sigmoid(gate)
    gate_act = (hidden_grad * up * sigmoid_gate * (1.0 + gate * (1.0 - sigmoid_gate))).astype(
        jnp.bfloat16
    )
    up_act = (hidden_grad * jax.nn.silu(gate)).astype(jnp.bfloat16)
    back_gate = jnp.einsum(
        "nch,ckbh->nckb", gate_act, gate_blocks, preferred_element_type=jnp.float32
    )
    back_up = jnp.einsum("nch,ckbh->nckb", up_act, up_blocks, preferred_element_type=jnp.float32)
    column_ids = jnp.arange(column_count, dtype=jnp.int32)[:, None]
    input_terms = jnp.zeros((token_count, column_count, row_blocks, block_size), jnp.float32)
    input_terms = (
        input_terms.at[:, column_ids, gate_rows]
        .add(back_gate)
        .at[:, column_ids, up_rows]
        .add(back_up)
    )
    input_narrow = input_terms.astype(jnp.bfloat16).reshape(
        token_count, column_count, shard_count, owned_width
    )
    input_arrived = lax.all_to_all(input_narrow, "shard", split_axis=2, concat_axis=2, tiled=True)
    tokens_grad = jnp.sum(input_arrived.astype(jnp.float32), axis=(1, 2)).astype(jnp.bfloat16)
    gate_term = jnp.einsum("nckb,nch->ckbh", gate_in, gate_act, preferred_element_type=jnp.float32)
    up_term = jnp.einsum("nckb,nch->ckbh", up_in, up_act, preferred_element_type=jnp.float32)
    down_term = jnp.einsum(
        cot_form + ",nch->cojhb", cot_five, hidden, preferred_element_type=jnp.float32
    )
    down_term = down_term.reshape(column_count, nonzero, block_size, block_size)
    gate_sum, up_sum, down_sum = (
        lax.psum_scatter(
            gate_term.astype(jnp.bfloat16), ("dp", "tok"), scatter_dimension=1, tiled=True
        ).astype(jnp.float32),
        lax.psum_scatter(
            up_term.astype(jnp.bfloat16), ("dp", "tok"), scatter_dimension=1, tiled=True
        ).astype(jnp.float32),
        lax.psum_scatter(
            down_term.astype(jnp.bfloat16), ("dp", "tok"), scatter_dimension=1, tiled=True
        ).astype(jnp.float32),
    )
    return (
        mixed,
        tokens_grad,
        gate_sum.astype(jnp.bfloat16),
        up_sum.astype(jnp.bfloat16),
        down_sum.astype(jnp.bfloat16),
    )


def solution(mesh):
    in_specs = (
        P(("groups", "dp", "tok"), "shard"),
        P("shard", None, None, None),
        P("shard", None, None, None),
        P("shard", None, None, None),
        P("shard", None),
        P("shard", None),
        P(),
        P(("groups", "dp", "tok"), "shard"),
    )
    out_specs = (
        P(("groups", "dp", "tok"), "shard"),
        P(("groups", "dp", "tok"), "shard"),
        P(("groups", "shard"), ("dp", "tok"), None, None),
        P(("groups", "shard"), ("dp", "tok"), None, None),
        P(("groups", "shard"), ("dp", "tok"), None, None),
    )
    return jax.shard_map(body, mesh=mesh, in_specs=in_specs, out_specs=out_specs, check_vma=False)
```

profile of v0, /device:TPU:0, one launch (start us, length us, event | category | flops | bytes accessed | tf_op | source)
XLA Modules:
  0.0 281.4 jit_solution(18129311782604778208)
XLA Ops:
  7.2 2.1 copy.53
  11.8 2.1 gather_fusion
  14.0 3.3 %copy.66 = bf16[256,32,128]{0,2,1:T(8,128)(2,1)S(1)} copy(bf16[256,32,128]{2,0,1:T(8,128)(2,1)} %bitcast.152) | data formatting | bytes 4194304 | tf_op jit(solution)/shard_map/jit(_take)/gather | solution.py:43
  17.4 1.7 bitcast_select_fusion
  19.1 6.5 %all-to-all-start.1 = ((bf16[256,4,1024]{0,2,1:T(8,128)(2,1)}), bf16[256,4,1024]{0,2,1:T(8,128)(2,1)}, u32[]{:S(2)}, u32[]{:S(2)}) async-start(bf16[256,4,1024]{0,2,1:T(8,128)(2,1)} %bitcast_select_fusion), calls=%async_computation.1 | async-start | bytes 4194304 | tf_op jit(solution)/shard_map/all_to_all | solution.py:45
  27.6 68.2 %all-gather.2.cloned.1.call-done = bf16[256,4096]{0,1:T(8,128)(2,1)} async-done(((bf16[256,1024]{0,1:T(8,128)(2,1)}), bf16[256,4096]{0,1:T(8,128)(2,1)}) %all-gather.2.cloned.1.call-update) | async-done | bytes 2097168 | tf_op jit(solution)/shard_map/all_gather | solution.py:17
  95.8 3.2 %copy.54 = bf16[256,32,128]{2,0,1:T(8,128)(2,1)S(1)} copy(bf16[256,32,128]{0,2,1:T(8,128)(2,1)} %bitcast.156) | data formatting | bytes 4194304 | tf_op jit(solution)/shard_map/reshape | solution.py:19
  99.0 2.1 gather_fusion.1
  101.1 3.9 %copy.55 = bf16[2,16,256,128]{2,3,1,0:T(8,128)(2,1)} copy(bf16[2,16,256,128]{3,2,1,0:T(8,128)(2,1)} %bitcast.150) | data formatting | bytes 4194304 | tf_op jit(solution)/shard_map/jit(_take)/gather | solution.py:20
  105.0 2.1 gather_fusion.2
  107.2 4.0 %copy.58 = bf16[2,16,256,128]{2,3,1,0:T(8,128)(2,1)} copy(bf16[2,16,256,128]{3,2,1,0:T(8,128)(2,1)} %bitcast.149) | data formatting | bytes 4194304 | tf_op jit(solution)/shard_map/jit(_take)/gather | solution.py:21
  111.2 2.7 convolution_bitcast_fusion.1
  119.2 3.9 %all-to-all-start = ((bf16[256,2,4,512]{0,3,1,2:T(8,128)(2,1)}), bf16[256,2,4,512]{0,3,1,2:T(8,128)(2,1)S(1)}, u32[]{:S(2)}, u32[]{:S(2)}) async-start(bf16[256,2,4,512]{0,3,1,2:T(8,128)(2,1)} %copy.61), calls=%async_computation | async-start | bytes 4194304 | tf_op jit(solution)/shard_map/all_to_all | solution.py:29
  124.5 3.9 %fusion.35 = f32[2,256,16,128]{3,1,2,0:T(8,128)} fusion(bf16[2,16,128,128]{3,2,1,0:T(8,128)(2,1)} %param.11, bf16[256,2,128]{2,0,1:T(8,128)(2,1)S(1)} %get-tuple-element.15), kind=kOutput, calls=%fused_computation.40 | convolution fusion | flops 268435456 | bytes 5373952 | tf_op jit(solution)/shard_map/nch,ckbh->nckb/dot_general | solution.py:57
  128.4 4.3 %broadcast_in_dim.45 = f32[256,2,32,128]{3,0,2,1:T(8,128)} broadcast(f32[]{:T(128)} %constant.30.clone.1), dimensions={} | broadcast | bytes 8388612 | tf_op jit(solution)/shard_map/broadcast_in_dim | solution.py:62
  132.7 10.4 %scatter_fusion = f32[256,2,32,128]{3,0,2,1:T(8,128)} fusion(f32[256,2,32,128]{3,0,2,1:T(8,128)} %broadcast_in_dim.45, s32[32]{0:T(128)S(1)} %reshape.118, f32[32,256,128]{2,1,0:T(8,128)} %bitcast.143), kind=kCustom, calls=%fused_computation.3 | custom fusion | flops 1048576 | bytes 12583168 | tf_op jit(solution)/shard_map/scatter-add | solution.py:65
  143.1 2.7 fusion.51
  145.8 10.4 %scatter_fusion.1 = f32[256,2,32,128]{3,0,2,1:T(8,128)} fusion(f32[256,2,32,128]{3,0,2,1:T(8,128)} %scatter_fusion, s32[32]{0:T(128)S(1)} %reshape.124, f32[32,256,128]{2,1,0:T(8,128)} %bitcast.144), kind=kCustom, calls=%fused_computation.4 | custom fusion | flops 1048576 | bytes 12583168 | tf_op jit(solution)/shard_map/scatter-add | solution.py:67
  156.2 6.1 %convert_element_type.59 = bf16[256,2,32,128]{3,0,2,1:T(8,128)(2,1)} convert(f32[256,2,32,128]{3,0,2,1:T(8,128)} %scatter_fusion.1) | non-fusion elementwise | flops 2097152 | bytes 12582912 | tf_op jit(solution)/shard_map/convert_element_type | solution.py:69
  162.2 6.4 %copy.69 = bf16[256,2,32,128]{0,3,2,1:T(8,128)(2,1)} copy(bf16[256,2,32,128]{3,0,2,1:T(8,128)(2,1)} %convert_element_type.59) | data formatting | bytes 8388608 | tf_op jit(solution)/shard_map/convert_element_type | solution.py:69
  168.6 4.4 %copy.70 = bf16[256,2,4,1024]{0,3,1,2:T(8,128)(2,1)} copy(bf16[256,2,4,1024]{0,3,2,1:T(8,128)(2,1)} %bitcast.146) | data formatting | bytes 8388608 | tf_op jit(solution)/shard_map/reshape | solution.py:69
  173.0 4.9 %all-to-all-start.2 = ((bf16[256,2,4,1024]{0,3,1,2:T(8,128)(2,1)}), bf16[256,2,4,1024]{0,3,1,2:T(8,128)(2,1)}, u32[]{:S(2)}, u32[]{:S(2)}) async-start(bf16[256,2,4,1024]{0,3,1,2:T(8,128)(2,1)} %copy.70), calls=%async_computation.2 | async-start | bytes 8388608 | tf_op jit(solution)/shard_map/all_to_all | solution.py:72
  178.0 3.6 %fusion.16 = bf16[2,128,4,4,128]{4,1,3,2,0:T(8,128)(2,1)} fusion(bf16[256,4,2,4,128]{0,4,3,2,1:T(8,128)(2,1)} %bitcast.29, bf16[256,2,128]{2,0,1:T(8,128)(2,1)S(1)} %get-tuple-element.16), kind=kOutput, calls=%fused_computation.20 | convolution fusion | flops 268959744 | bytes 3276800 | tf_op jit(solution)/shard_map/nocjb,nch->cojhb/dot_general | solution.py:76
  181.6 1.8 fusion.10
  183.4 1.8 fusion.13
  187.0 68.0 %all-reduce.6.cloned.1.call-done = (bf16[2,16,128,128]{3,2,1,0:T(8,128)(2,1)}, bf16[2,16,128,128]{3,2,1,0:T(8,128)(2,1)}, bf16[2,16,128,128]{3,2,1,0:T(8,128)(2,1)}) async-done(((bf16[2,16,128,128]{3,2,1,0:T(8,128)(2,1)}, bf16[2,16,128,128]{3,2,1,0:T(8,128)(2,1)}, bf16[2,16,128,128]{3,2,1,0:T(8,128)(2,1)}), (bf16[2,16,128,128]{3,2,1,0:T(8,128)(2,1)}, bf16[2,16,128,128]{3,2,1,0:T(8,128)(2,1)}, ...) | async-done | bytes 3145744
  255.0 1.7 constant_dynamic-slice_fusion.2
  256.7 1.9 constant_dynamic-slice_fusion
  258.6 3.2 %copy.63 = bf16[256,2,4,4,128]{4,2,3,0,1:T(4,128)(2,1)} copy(bf16[256,2,4,4,128]{0,4,3,1,2:T(8,128)(2,1)S(1)} %bitcast.151) | data formatting | bytes 4194304 | tf_op jit(solution)/shard_map/reshape | solution.py:30
  261.7 3.2 %fusion.19 = bf16[8,256,128]{2,0,1:T(8,128)(2,1)S(1)} fusion(bf16[256,2,4,4,128]{4,2,3,0,1:T(4,128)(2,1)} %copy.63, s32[4,2,4]{0,2,1:T(4,128)S(1)} %copy.52), kind=kOutput, calls=%fused_computation.22 | convolution fusion | flops 17039616 | bytes 2621568 | tf_op jit(solution)/shard_map/ncsjb,scjr->nrb/dot_general | solution.py:38
  265.9 4.7 %all-to-all-done.2 = bf16[256,2,4,1024]{0,3,1,2:T(8,128)(2,1)} async-done(((bf16[256,2,4,1024]{0,3,1,2:T(8,128)(2,1)}), bf16[256,2,4,1024]{0,3,1,2:T(8,128)(2,1)}, u32[]{:S(2)}, u32[]{:S(2)}) %all-to-all-start.2) | async-done | bytes 4194336 | tf_op jit(solution)/shard_map/all_to_all | solution.py:72
  270.5 3.0 %reduce_sum.12 = bf16[256,1024]{0,1:T(8,128)(2,1)S(1)} reduce(bf16[256,2,4,1024]{0,3,1,2:T(8,128)(2,1)} %all-to-all-done.2, bf16[]{:T(256)} %constant.52.clone.1), dimensions={1,2}, to_apply=%region_2.4 | reduce | flops 1835008 | bytes 4718594 | tf_op jit(solution)/shard_map/reduce_sum | solution.py:73
  (74 shorter events, 14.5 us)
Async XLA Ops:
  7.2 107.8 %copy-start = (bf16[2,16,128,128]{3,2,1,0:T(8,128)(2,1)S(1)}, bf16[2,16,128,128]{3,2,1,0:T(8,128)(2,1)}, u32[]{:S(2)}) copy-start(bf16[2,16,128,128]{3,2,1,0:T(8,128)(2,1)} %param.12) | copy-start | bytes 3145732
  7.2 88.6 %all-gather.2.cloned.1.call-start = ((), (), s32[]{:S(2)}) async-start(), calls=%async_computation.3 | async-start | bytes 2621440 | tf_op jit(solution)/shard_map/all_gather | solution.py:17
  19.1 6.5 %copy-start.10 = (s32[2,16]{1,0:T(2,128)S(1)}, s32[2,16]{1,0:T(2,128)}, u32[]{:S(2)}) copy-start(s32[2,16]{1,0:T(2,128)} %param.14) | copy-start | bytes 388
  19.1 6.6 %copy-start.11 = (s32[2,16]{1,0:T(2,128)S(1)}, s32[2,16]{1,0:T(2,128)}, u32[]{:S(2)}) copy-start(s32[2,16]{1,0:T(2,128)} %param.15) | copy-start | bytes 388
  19.1 6.7 %copy-start.2 = (bf16[2,16,128,128]{3,2,1,0:T(8,128)(2,1)S(1)}, bf16[2,16,128,128]{3,2,1,0:T(8,128)(2,1)}, u32[]{:S(2)}) copy-start(bf16[2,16,128,128]{3,2,1,0:T(8,128)(2,1)} %param.13) | copy-start | bytes 3145732
  19.1 92.1 %all-to-all-start.1 = ((bf16[256,4,1024]{0,2,1:T(8,128)(2,1)}), bf16[256,4,1024]{0,2,1:T(8,128)(2,1)}, u32[]{:S(2)}, u32[]{:S(2)}) async-start(bf16[256,4,1024]{0,2,1:T(8,128)(2,1)} %bitcast_select_fusion), calls=%async_computation.1 | async-start | bytes 4194304 | tf_op jit(solution)/shard_map/all_to_all | solution.py:45
  27.1 86.8 %copy-start.16 = (pred[2,16]{1,0:T(4,128)(4,1)}, pred[2,16]{1,0:T(4,128)(4,1)S(1)}, u32[]{:S(2)}) copy-start(pred[2,16]{1,0:T(4,128)(4,1)S(1)} %compare_and_fusion.1) | copy-start | bytes 100
  107.2 4.0 %copy-start.3 = (bf16[2,16,128,128]{3,2,1,0:T(8,128)(2,1)S(1)}, bf16[2,16,128,128]{3,2,1,0:T(8,128)(2,1)}, u32[]{:S(2)}) copy-start(bf16[2,16,128,128]{3,2,1,0:T(8,128)(2,1)} %param.13) | copy-start | bytes 3145732
  111.2 2.7 copy-start.9
  111.2 2.7 copy-start.5
  113.9 1.6 copy-start.7
  113.9 1.6 copy-start.14
  115.5 1.2 copy-start.4
  119.2 5.3 %copy-start.12 = (s32[2,16]{1,0:T(2,128)S(1)}, s32[2,16]{1,0:T(2,128)}, u32[]{:S(2)}) copy-start(s32[2,16]{1,0:T(2,128)} %param.15) | copy-start | bytes 388
  119.2 53.8 %all-to-all-start = ((bf16[256,2,4,512]{0,3,1,2:T(8,128)(2,1)}), bf16[256,2,4,512]{0,3,1,2:T(8,128)(2,1)S(1)}, u32[]{:S(2)}, u32[]{:S(2)}) async-start(bf16[256,2,4,512]{0,3,1,2:T(8,128)(2,1)} %copy.61), calls=%async_computation | async-start | bytes 4194304 | tf_op jit(solution)/shard_map/all_to_all | solution.py:29
  173.0 97.5 %all-to-all-start.2 = ((bf16[256,2,4,1024]{0,3,1,2:T(8,128)(2,1)}), bf16[256,2,4,1024]{0,3,1,2:T(8,128)(2,1)}, u32[]{:S(2)}, u32[]{:S(2)}) async-start(bf16[256,2,4,1024]{0,3,1,2:T(8,128)(2,1)} %copy.70), calls=%async_computation.2 | async-start | bytes 8388608 | tf_op jit(solution)/shard_map/all_to_all | solution.py:72
  177.9 3.7 %copy-start.17 = (pred[2,16]{1,0:T(4,128)(4,1)S(1)}, pred[2,16]{1,0:T(4,128)(4,1)}, u32[]{:S(2)}) copy-start(pred[2,16]{1,0:T(4,128)(4,1)} %copy-done.16) | copy-start | bytes 100
  177.9 77.1 %all-reduce.6.cloned.1.call-start = ((), (), s32[]{:S(2)}) async-start(), calls=%async_computation.4 | async-start | bytes 6291456
  178.0 3.6 %copy-start.6 = (bf16[2,16,256,128]{2,3,1,0:T(8,128)(2,1)S(1)}, bf16[2,16,256,128]{2,3,1,0:T(8,128)(2,1)}, u32[]{:S(2)}) copy-start(bf16[2,16,256,128]{2,3,1,0:T(8,128)(2,1)} %copy.55) | copy-start | bytes 6291460
  181.6 1.8 copy-start.8
  181.6 1.8 copy-start.15
  185.1 0.7 copy-start.13
  265.0 9.6 %copy-start.1 = (bf16[2,16,128,128]{3,2,1,0:T(8,128)(2,1)S(1)}, bf16[2,16,128,128]{3,2,1,0:T(8,128)(2,1)}, u32[]{:S(2)}) copy-start(bf16[2,16,128,128]{3,2,1,0:T(8,128)(2,1)} %param.12) | copy-start | bytes 3145732
Sparse Core Ops, SparseCore 0:
  10.1 85.5 all-gather.1
  185.3 69.7 all-reduce.5
where the time goes:
time: 283 us; the launch traced here: 281 us
  waiting for transfers between devices  141 us (50%)
  local copies, waits for them, and re-layouts  54.1 us (19%)
  other arithmetic  33.8 us (12%)
  matrix products  22.5 us (8%)
  starting transfers between devices  15.3 us (5%)
  between operations  14.9 us (5%)
    all_gather x1, waiting for transfers between devices, body(): gathered = lax.all_gather(tokens, 'shard', axis=1, tiled=True)  68.2 us
    unnamed x3, waiting for transfers between devices  68.1 us
    scatter-add x2, other arithmetic, body(): input_terms = input_terms.at[:, column_ids, gate_rows].add(back_gate).at[...  20.7 us
    unnamed x46, local copies, waits for them, and re-layouts  12 us
    all_to_all x1, starting transfers between devices, body(): lax.all_to_all(outgoing, 'shard', split_axis=1, concat_axis=1, tiled=True)  6.48 us
    convert_element_type x1, local copies, waits for them, and re-layouts, body(): input_terms.astype(jnp.bfloat16)  6.38 us
    gather x2, local copies, waits for them, and re-layouts, body(): up_in = jnp.take(tokens3, up_rows, axis=1)  6.15 us
    convert_element_type x1, other arithmetic, body(): input_terms.astype(jnp.bfloat16)  6.09 us
  transfers between devices with their start and end apart: 5, of which 3 were waited for; matrix products, arithmetic and copies ran while one was open for 34% of the time, Pallas kernels for 0%

commit v1 on v0

--- a/solution.py
+++ b/solution.py
@@ -2,6 +2,28 @@
 import jax.numpy as jnp
 from jax import lax
 from jax.sharding import PartitionSpec as P
+
+
+def joined_along(blocks, dim):
+    shape = list(blocks.shape[1:])
+    shape[dim] *= blocks.shape[0]
+    return jnp.moveaxis(blocks, 0, dim).reshape(shape)
+
+
+def gather_around(x, axis, dim):
+    devices = lax.axis_size(axis)
+    pairs = [(i, (i + 1) % devices) for i in range(devices)]
+    back = [(b, a) for a, b in pairs]
+    lower, upper = ([], [])
+    for lap in range(devices - 1):
+        if lap % 2 == 0:
+            lower.append(lax.ppermute(lower[-1] if lower else x, axis, pairs))
+        else:
+            upper.append(lax.ppermute(upper[-1] if upper else x, axis, back))
+    pieces = jnp.stack([*lower[::-1], x, *upper])
+    shift = lax.axis_index(axis) - len(lower)
+    pieces = pieces[(jnp.arange(devices) - shift) % devices]
+    return joined_along(pieces, dim)
 
 
 def body(tokens, gate_blocks, up_blocks, down_blocks, gate_rows, up_rows, down_rows, cotangent):
@@ -14,7 +36,7 @@
     block_size = gate_blocks.shape[2]
     owned_blocks = owned_width // block_size
     per_owner = nonzero // shard_count
-    gathered = lax.all_gather(tokens, "shard", axis=1, tiled=True)
+    gathered = gather_around(tokens, "shard", 1)
     row_blocks = gathered.shape[1] // block_size
     tokens3 = gathered.reshape(token_count, row_blocks, block_size)
     gate_in = jnp.take(tokens3, gate_rows, axis=1)

time: 283 us -> 300 us (1.060)
  starting transfers between devices: 15.3 us -> 40.1 us
  waiting for transfers between devices: 141 us -> 126 us
  local copies, waits for them, and re-layouts: 54.1 us -> 57.4 us
    all_gather x1 -> x0, waiting for transfers between devices: 68.2 us -> none  [body(): gathered = lax.all_gather(tokens, 'shard', axis=1, tiled=True)]
    ppermute x0 -> x3, waiting for transfers between devices: none -> 54.7 us  [the longest x2 54.7 us: gather_around(): lower.append(lax.ppermute(lower[-1] if lower else x, axis, pairs))]
    ppermute x0 -> x3, starting transfers between devices: none -> 22.6 us  [the longest x2 20.8 us: gather_around(): lower.append(lax.ppermute(lower[-1] if lower else x, axis, pairs))]
    transpose x0 -> x1, local copies, waits for them, and re-layouts: none -> 3.93 us  [joined_along(): return jnp.moveaxis(blocks, 0, dim).reshape(shape)]
    another operation x0 -> x1, local copies, waits for them, and re-layouts: none -> 3.21 us  [body(): tokens3 = gathered.reshape(token_count, row_blocks, block_size)]
    reshape x1 -> x0, local copies, waits for them, and re-layouts: 3.21 us -> none  [body(): tokens3 = gathered.reshape(token_count, row_blocks, block_size)]
    unnamed x46 -> x49, local copies, waits for them, and re-layouts: 12 us -> 9.4 us
    unnamed x3 -> x2, waiting for transfers between devices: 68.1 us -> 68.2 us
  transfers between devices with their start and end apart: 5 -> 7, of which waited for: 3 -> 4; matrix products, arithmetic and copies ran while one was open for 34% -> 32% of each run, Pallas kernels for 0% -> 0%
where the time goes in v1:
time: 300 us; the launch traced here: 299 us
  waiting for transfers between devices  126 us (42%)
  local copies, waits for them, and re-layouts  57.4 us (19%)
  starting transfers between devices  40.1 us (13%)
  other arithmetic  35.4 us (12%)
  matrix products  24.8 us (8%)
  between operations  14.9 us (5%)
    unnamed x2, waiting for transfers between devices  68.2 us
    ppermute x2, waiting for transfers between devices, gather_around(): lower.append(lax.ppermute(lower[-1] if lower else x, axis, pairs))  54.7 us
    ppermute x2, starting transfers between devices, gather_around(): lower.append(lax.ppermute(lower[-1] if lower else x, axis, pairs))  20.8 us
    scatter-add x2, other arithmetic, body(): input_terms = input_terms.at[:, column_ids, gate_rows].add(back_gate).at[...  20.6 us
    unnamed x49, local copies, waits for them, and re-layouts  9.4 us
    all_to_all x1, starting transfers between devices, body(): lax.all_to_all(outgoing, 'shard', split_axis=1, concat_axis=1, tiled=True)  6.49 us
    convert_element_type x1, local copies, waits for them, and re-layouts, body(): input_terms.astype(jnp.bfloat16)  6.39 us
    gather x2, local copies, waits for them, and re-layouts, body(): up_in = jnp.take(tokens3, up_rows, axis=1)  6.16 us
  transfers between devices with their start and end apart: 7, of which 4 were waited for; matrix products, arithmetic and copies ran while one was open for 32% of the time, Pallas kernels for 0%

profile of v1, /device:TPU:0, one launch (start us, length us, event | category | flops | bytes accessed | tf_op | source)
XLA Modules:
  0.0 298.5 jit_solution(7360687809434688846)
XLA Ops:
  9.7 2.2 gather_fusion.1
  11.9 3.3 %copy.66 = bf16[256,32,128]{0,2,1:T(8,128)(2,1)S(1)} copy(bf16[256,32,128]{2,0,1:T(8,128)(2,1)} %bitcast.159) | data formatting | bytes 4194304 | tf_op jit(solution)/shard_map/jit(_take)/gather | solution.py:65
  17.0 6.5 %all-to-all-start.1 = ((bf16[256,4,1024]{0,2,1:T(8,128)(2,1)}), bf16[256,4,1024]{0,2,1:T(8,128)(2,1)}, u32[]{:S(2)}, u32[]{:S(2)}) async-start(bf16[256,4,1024]{0,2,1:T(8,128)(2,1)} %bitcast_select_fusion), calls=%async_computation.1 | async-start | bytes 4194304 | tf_op jit(solution)/shard_map/all_to_all | solution.py:67
  23.5 2.0 collective-permute-start
  28.8 45.2 %collective-permute-done = bf16[256,1024]{1,0:T(8,128)(2,1)S(1)} collective-permute-done((bf16[256,1024]{1,0:T(8,128)(2,1)S(1)}, bf16[256,1024]{1,0:T(8,128)(2,1)S(1)}, u32[]{:S(2)}, u32[]{:S(2)}) %collective-permute-start) | collective-permute-done | bytes 524320 | tf_op jit(solution)/shard_map/ppermute | solution.py:20
  74.0 18.8 %collective-permute-start.1 = (bf16[256,1024]{1,0:T(8,128)(2,1)S(1)}, bf16[256,1024]{1,0:T(8,128)(2,1)S(1)}, u32[]{:S(2)}, u32[]{:S(2)}) collective-permute-start(bf16[256,1024]{1,0:T(8,128)(2,1)S(1)} %collective-permute-done), channel_id=1, source_target_pairs={{0,4},{4,8},{8,12},{12,0},{1,5},{5,9},{9,13},{13,1},{2,6},{6,10},{... | collective-permute-start | bytes 1572872 | tf_op jit(solution)/shard_map/ppermute | solution.py:20
  93.3 9.5 %collective-permute-done.1 = bf16[256,1024]{1,0:T(8,128)(2,1)S(1)} collective-permute-done((bf16[256,1024]{1,0:T(8,128)(2,1)S(1)}, bf16[256,1024]{1,0:T(8,128)(2,1)S(1)}, u32[]{:S(2)}, u32[]{:S(2)}) %collective-permute-start.1) | collective-permute-done | bytes 524320 | tf_op jit(solution)/shard_map/ppermute | solution.py:20
  104.5 2.0 gather_fusion
  106.4 3.9 %copy.53 = bf16[256,4,1024]{0,2,1:T(8,128)(2,1)} copy(bf16[256,4,1024]{2,0,1:T(8,128)(2,1)} %bitcast.160) | data formatting | bytes 4194304 | tf_op jit(solution)/shard_map/transpose | solution.py:10
  110.4 3.2 %copy.54 = bf16[256,32,128]{2,0,1:T(8,128)(2,1)S(1)} copy(bf16[256,32,128]{0,2,1:T(8,128)(2,1)} %bitcast.161) | data formatting | bytes 4194304 | tf_op jit(solution)/shard_map/reshape;reshape | solution.py:41
  113.6 2.1 gather_fusion.2
  115.7 3.9 %copy.55 = bf16[2,16,256,128]{2,3,1,0:T(8,128)(2,1)} copy(bf16[2,16,256,128]{3,2,1,0:T(8,128)(2,1)} %bitcast.157) | data formatting | bytes 4194304 | tf_op jit(solution)/shard_map/jit(_take)/gather | solution.py:42
  119.7 2.1 gather_fusion.3
  121.8 4.0 %copy.58 = bf16[2,16,256,128]{2,3,1,0:T(8,128)(2,1)} copy(bf16[2,16,256,128]{3,2,1,0:T(8,128)(2,1)} %bitcast.156) | data formatting | bytes 4194304 | tf_op jit(solution)/shard_map/jit(_take)/gather | solution.py:43
  125.8 3.4 %fusion.20 = f32[256,2,128]{2,0,1:T(8,128)} fusion(bf16[2,16,128,128]{3,2,1,0:T(8,128)(2,1)S(1)} %copy-done.8, bf16[2,16,256,128]{2,3,1,0:T(8,128)(2,1)} %copy.55, pred[2,16]{1,0:T(4,128)(4,1)S(1)} %compare_and_fusion.1), kind=kOutput, calls=%fused_computation.26 | convolution fusion | flops 269484032 | bytes 3407904 | tf_op jit(solution)/shard_map/nckb,ckbh->nch/dot_general | solution.py:44
  129.3 2.7 convolution_bitcast_fusion.1
  135.7 5.8 %all-to-all-start = ((bf16[256,2,4,512]{0,3,1,2:T(8,128)(2,1)}), bf16[256,2,4,512]{0,3,1,2:T(8,128)(2,1)S(1)}, u32[]{:S(2)}, u32[]{:S(2)}) async-start(bf16[256,2,4,512]{0,3,1,2:T(8,128)(2,1)} %copy.61), calls=%async_computation | async-start | bytes 4194304 | tf_op jit(solution)/shard_map/all_to_all | solution.py:51
  142.9 3.9 %fusion.35 = f32[2,256,16,128]{3,1,2,0:T(8,128)} fusion(bf16[2,16,128,128]{3,2,1,0:T(8,128)(2,1)} %param.11, bf16[256,2,128]{2,0,1:T(8,128)(2,1)S(1)} %get-tuple-element.15), kind=kOutput, calls=%fused_computation.42 | convolution fusion | flops 268435456 | bytes 5373952 | tf_op jit(solution)/shard_map/nch,ckbh->nckb/dot_general | solution.py:79
  146.8 4.3 %broadcast_in_dim.46 = f32[256,2,32,128]{3,0,2,1:T(8,128)} broadcast(f32[]{:T(128)} %constant.65.clone.1), dimensions={} | broadcast | bytes 8388612 | tf_op jit(solution)/shard_map/broadcast_in_dim | solution.py:84
  151.1 10.3 %scatter_fusion = f32[256,2,32,128]{3,0,2,1:T(8,128)} fusion(f32[256,2,32,128]{3,0,2,1:T(8,128)} %broadcast_in_dim.46, s32[32]{0:T(128)S(1)} %reshape.171, f32[32,256,128]{2,1,0:T(8,128)} %bitcast.150), kind=kCustom, calls=%fused_computation.4 | custom fusion | flops 1048576 | bytes 12583168 | tf_op jit(solution)/shard_map/scatter-add | solution.py:87
  161.4 2.7 fusion.53
  164.1 10.3 %scatter_fusion.1 = f32[256,2,32,128]{3,0,2,1:T(8,128)} fusion(f32[256,2,32,128]{3,0,2,1:T(8,128)} %scatter_fusion, s32[32]{0:T(128)S(1)} %reshape.177, f32[32,256,128]{2,1,0:T(8,128)} %bitcast.151), kind=kCustom, calls=%fused_computation.5 | custom fusion | flops 1048576 | bytes 12583168 | tf_op jit(solution)/shard_map/scatter-add | solution.py:89
  174.4 6.1 %convert_element_type.59 = bf16[256,2,32,128]{3,0,2,1:T(8,128)(2,1)} convert(f32[256,2,32,128]{3,0,2,1:T(8,128)} %scatter_fusion.1) | non-fusion elementwise | flops 2097152 | bytes 12582912 | tf_op jit(solution)/shard_map/convert_element_type | solution.py:91
  180.5 6.4 %copy.69 = bf16[256,2,32,128]{0,3,2,1:T(8,128)(2,1)} copy(bf16[256,2,32,128]{3,0,2,1:T(8,128)(2,1)} %convert_element_type.59) | data formatting | bytes 8388608 | tf_op jit(solution)/shard_map/convert_element_type | solution.py:91
  186.9 4.4 %copy.70 = bf16[256,2,4,1024]{0,3,1,2:T(8,128)(2,1)} copy(bf16[256,2,4,1024]{0,3,2,1:T(8,128)(2,1)} %bitcast.153) | data formatting | bytes 8388608 | tf_op jit(solution)/shard_map/reshape | solution.py:91
  191.3 5.2 %all-to-all-start.2 = ((bf16[256,2,4,1024]{0,3,1,2:T(8,128)(2,1)}), bf16[256,2,4,1024]{0,3,1,2:T(8,128)(2,1)}, u32[]{:S(2)}, u32[]{:S(2)}) async-start(bf16[256,2,4,1024]{0,3,1,2:T(8,128)(2,1)} %copy.70), calls=%async_computation.2 | async-start | bytes 8388608 | tf_op jit(solution)/shard_map/all_to_all | solution.py:94
  196.5 3.6 %fusion.16 = bf16[2,128,4,4,128]{4,1,3,2,0:T(8,128)(2,1)} fusion(bf16[256,4,2,4,128]{0,4,3,2,1:T(8,128)(2,1)} %bitcast.35, bf16[256,2,128]{2,0,1:T(8,128)(2,1)S(1)} %get-tuple-element.16), kind=kOutput, calls=%fused_computation.22 | convolution fusion | flops 268959744 | bytes 3276800 | tf_op jit(solution)/shard_map/nocjb,nch->cojhb/dot_general | solution.py:98
  205.6 68.2 %all-reduce.6.cloned.1.call-done = (bf16[2,16,128,128]{3,2,1,0:T(8,128)(2,1)}, bf16[2,16,128,128]{3,2,1,0:T(8,128)(2,1)}, bf16[2,16,128,128]{3,2,1,0:T(8,128)(2,1)}) async-done(((bf16[2,16,128,128]{3,2,1,0:T(8,128)(2,1)}, bf16[2,16,128,128]{3,2,1,0:T(8,128)(2,1)}, bf16[2,16,128,128]{3,2,1,0:T(8,128)(2,1)}), (bf16[2,16,128,128]{3,2,1,0:T(8,128)(2,1)}, bf16[2,16,128,128]{3,2,1,0:T(8,128)(2,1)}, ...) | async-done | bytes 3145744
  277.3 3.2 %copy.63 = bf16[256,2,4,4,128]{4,2,3,0,1:T(4,128)(2,1)} copy(bf16[256,2,4,4,128]{0,4,3,1,2:T(8,128)(2,1)S(1)} %bitcast.158) | data formatting | bytes 4194304 | tf_op jit(solution)/shard_map/reshape | solution.py:52
  280.5 3.2 %fusion.19 = bf16[8,256,128]{2,0,1:T(8,128)(2,1)S(1)} fusion(bf16[256,2,4,4,128]{4,2,3,0,1:T(4,128)(2,1)} %copy.63, s32[4,2,4]{0,2,1:T(4,128)S(1)} %copy.52), kind=kOutput, calls=%fused_computation.24 | convolution fusion | flops 17039616 | bytes 2621568 | tf_op jit(solution)/shard_map/ncsjb,scjr->nrb/dot_general | solution.py:60
  284.6 3.0 %all-to-all-done.2 = bf16[256,2,4,1024]{0,3,1,2:T(8,128)(2,1)} async-done(((bf16[256,2,4,1024]{0,3,1,2:T(8,128)(2,1)}), bf16[256,2,4,1024]{0,3,1,2:T(8,128)(2,1)}, u32[]{:S(2)}, u32[]{:S(2)}) %all-to-all-start.2) | async-done | bytes 4194336 | tf_op jit(solution)/shard_map/all_to_all | solution.py:94
  287.6 3.0 %reduce_sum.12 = bf16[256,1024]{0,1:T(8,128)(2,1)S(1)} reduce(bf16[256,2,4,1024]{0,3,1,2:T(8,128)(2,1)} %all-to-all-done.2, bf16[]{:T(256)} %constant.69.clone.1), dimensions={1,2}, to_apply=%region_2.4 | reduce | flops 1835008 | bytes 4718594 | tf_op jit(solution)/shard_map/reduce_sum | solution.py:95
  (85 shorter events, 25.1 us)
Async XLA Ops:
  7.2 124.8 %copy-start = (bf16[2,16,128,128]{3,2,1,0:T(8,128)(2,1)S(1)}, bf16[2,16,128,128]{3,2,1,0:T(8,128)(2,1)}, u32[]{:S(2)}) copy-start(bf16[2,16,128,128]{3,2,1,0:T(8,128)(2,1)} %param.12) | copy-start | bytes 3145732
  17.0 6.5 %copy-start.9 = (bf16[256,1024]{1,0:T(8,128)(2,1)S(1)}, bf16[256,1024]{1,0:T(8,128)(2,1)}, u32[]{:S(2)}) copy-start(bf16[256,1024]{1,0:T(8,128)(2,1)} %param.10) | copy-start | bytes 1572868
  17.0 10.3 %copy-start.11 = (s32[2,16]{1,0:T(2,128)S(1)}, s32[2,16]{1,0:T(2,128)}, u32[]{:S(2)}) copy-start(s32[2,16]{1,0:T(2,128)} %param.14) | copy-start | bytes 388
  17.0 10.4 %copy-start.12 = (s32[2,16]{1,0:T(2,128)S(1)}, s32[2,16]{1,0:T(2,128)}, u32[]{:S(2)}) copy-start(s32[2,16]{1,0:T(2,128)} %param.15) | copy-start | bytes 388
  17.0 10.5 %copy-start.2 = (bf16[2,16,128,128]{3,2,1,0:T(8,128)(2,1)S(1)}, bf16[2,16,128,128]{3,2,1,0:T(8,128)(2,1)}, u32[]{:S(2)}) copy-start(bf16[2,16,128,128]{3,2,1,0:T(8,128)(2,1)} %param.13) | copy-start | bytes 3145732
  17.0 112.3 %all-to-all-start.1 = ((bf16[256,4,1024]{0,2,1:T(8,128)(2,1)}), bf16[256,4,1024]{0,2,1:T(8,128)(2,1)}, u32[]{:S(2)}, u32[]{:S(2)}) async-start(bf16[256,4,1024]{0,2,1:T(8,128)(2,1)} %bitcast_select_fusion), calls=%async_computation.1 | async-start | bytes 4194304 | tf_op jit(solution)/shard_map/all_to_all | solution.py:67
  23.5 50.5 %collective-permute-start = (bf16[256,1024]{1,0:T(8,128)(2,1)S(1)}, bf16[256,1024]{1,0:T(8,128)(2,1)S(1)}, u32[]{:S(2)}, u32[]{:S(2)}) collective-permute-start(bf16[256,1024]{1,0:T(8,128)(2,1)S(1)} %copy-done.9), channel_id=1, source_target_pairs={{0,4},{4,8},{8,12},{12,0},{1,5},{5,9},{9,13},{13,1},{2,6},{6,10},{... | collective-permute-start | bytes 1572872 | tf_op jit(solution)/shard_map/ppermute | solution.py:20
  25.5 67.8 %collective-permute-start.2 = (bf16[256,1024]{1,0:T(8,128)(2,1)S(1)}, bf16[256,1024]{1,0:T(8,128)(2,1)}, u32[]{:S(2)}, u32[]{:S(2)}) collective-permute-start(bf16[256,1024]{1,0:T(8,128)(2,1)S(1)} %copy-done.9), channel_id=1, source_target_pairs={{4,0},{8,4},{12,8},{0,12},{5,1},{9,5},{13,9},{1,13},{6,2},{10,6},{... | collective-permute-start | bytes 1572872 | tf_op jit(solution)/shard_map/ppermute | solution.py:22
  74.0 28.8 %copy-start.10 = (bf16[256,1024]{1,0:T(8,128)(2,1)}, bf16[256,1024]{1,0:T(8,128)(2,1)S(1)}, u32[]{:S(2)}) copy-start(bf16[256,1024]{1,0:T(8,128)(2,1)S(1)} %collective-permute-done) | copy-start | bytes 1572868
  74.0 28.8 %collective-permute-start.1 = (bf16[256,1024]{1,0:T(8,128)(2,1)S(1)}, bf16[256,1024]{1,0:T(8,128)(2,1)S(1)}, u32[]{:S(2)}, u32[]{:S(2)}) collective-permute-start(bf16[256,1024]{1,0:T(8,128)(2,1)S(1)} %collective-permute-done), channel_id=1, source_target_pairs={{0,4},{4,8},{8,12},{12,0},{1,5},{5,9},{9,13},{13,1},{2,6},{6,10},{... | collective-permute-start | bytes 1572872 | tf_op jit(solution)/shard_map/ppermute | solution.py:20
  92.8 33.0 %copy-start.17 = (pred[2,16]{1,0:T(4,128)(4,1)}, pred[2,16]{1,0:T(4,128)(4,1)S(1)}, u32[]{:S(2)}) copy-start(pred[2,16]{1,0:T(4,128)(4,1)S(1)} %compare_and_fusion.1) | copy-start | bytes 100
  121.8 4.0 %copy-start.8 = (bf16[2,16,128,128]{3,2,1,0:T(8,128)(2,1)S(1)}, bf16[2,16,128,128]{3,2,1,0:T(8,128)(2,1)}, u32[]{:S(2)}) copy-start(bf16[2,16,128,128]{3,2,1,0:T(8,128)(2,1)} %param.11) | copy-start | bytes 3145732
  125.8 3.4 %copy-start.3 = (bf16[2,16,128,128]{3,2,1,0:T(8,128)(2,1)S(1)}, bf16[2,16,128,128]{3,2,1,0:T(8,128)(2,1)}, u32[]{:S(2)}) copy-start(bf16[2,16,128,128]{3,2,1,0:T(8,128)(2,1)} %param.13) | copy-start | bytes 3145732
  129.2 2.7 copy-start.15
  129.2 2.7 copy-start.19
  129.3 2.7 copy-start.6
  132.0 1.2 copy-start.4
  135.7 7.1 %copy-start.13 = (s32[2,16]{1,0:T(2,128)S(1)}, s32[2,16]{1,0:T(2,128)}, u32[]{:S(2)}) copy-start(s32[2,16]{1,0:T(2,128)} %param.15) | copy-start | bytes 388
  135.7 55.7 %all-to-all-start = ((bf16[256,2,4,512]{0,3,1,2:T(8,128)(2,1)}), bf16[256,2,4,512]{0,3,1,2:T(8,128)(2,1)S(1)}, u32[]{:S(2)}, u32[]{:S(2)}) async-start(bf16[256,2,4,512]{0,3,1,2:T(8,128)(2,1)} %copy.61), calls=%async_computation | async-start | bytes 4194304 | tf_op jit(solution)/shard_map/all_to_all | solution.py:51
  191.3 96.3 %all-to-all-start.2 = ((bf16[256,2,4,1024]{0,3,1,2:T(8,128)(2,1)}), bf16[256,2,4,1024]{0,3,1,2:T(8,128)(2,1)}, u32[]{:S(2)}, u32[]{:S(2)}) async-start(bf16[256,2,4,1024]{0,3,1,2:T(8,128)(2,1)} %copy.70), calls=%async_computation.2 | async-start | bytes 8388608 | tf_op jit(solution)/shard_map/all_to_all | solution.py:94
  196.5 3.6 %copy-start.18 = (pred[2,16]{1,0:T(4,128)(4,1)S(1)}, pred[2,16]{1,0:T(4,128)(4,1)}, u32[]{:S(2)}) copy-start(pred[2,16]{1,0:T(4,128)(4,1)} %copy-done.17) | copy-start | bytes 100
  196.5 77.3 %all-reduce.6.cloned.1.call-start = ((), (), s32[]{:S(2)}) async-start(), calls=%async_computation.3 | async-start | bytes 6291456
  196.5 3.6 %copy-start.5 = (bf16[2,16,256,128]{2,3,1,0:T(8,128)(2,1)S(1)}, bf16[2,16,256,128]{2,3,1,0:T(8,128)(2,1)}, u32[]{:S(2)}) copy-start(bf16[2,16,256,128]{2,3,1,0:T(8,128)(2,1)} %copy.55) | copy-start | bytes 6291460
  200.1 1.8 copy-start.7
  200.1 1.8 copy-start.16
  203.7 0.7 copy-start.14
  283.7 8.0 %copy-start.1 = (bf16[2,16,128,128]{3,2,1,0:T(8,128)(2,1)S(1)}, bf16[2,16,128,128]{3,2,1,0:T(8,128)(2,1)}, u32[]{:S(2)}) copy-start(bf16[2,16,128,128]{3,2,1,0:T(8,128)(2,1)} %param.12) | copy-start | bytes 3145732
Sparse Core Ops, SparseCore 0:
  203.8 69.9 all-reduce.5
